TPU v7x, 32 devices: a whole 2x2x4 slice. The times are simulated.
32 devices in a mesh: date: 2 (over y), slab: 16 (over z, x, core).
Axes of the slice: x: 2, y: 2, z: 4, core: 2. Of those that a mesh axis runs over, the one named last changes fastest.
Arguments:
- pressure: float32 [16, 12288], P('slab', 'date'), parts along dimension 1, may hold values from -6 to 6
- density: float32 [16, 12288], P('slab', 'date'), parts along dimension 1, may hold values from -6 to 6
- vertical_wind: float32 [16, 12288], P('slab', 'date'), parts along dimension 1, may hold values from -6 to 6
- horizontal_wind: float32 [2, 16, 12288], P(None, 'slab', 'date'), parts along dimension 2, may hold values from -6 to 6
- metric_terms: float32 [2, 6144], replicated, may hold values from 0.25 to 1
- neighbors: int32 [4, 6144], replicated, may hold values from 0 to 6143, as said below
- level_order: int32 [16], replicated, may hold values from 0 to 15, each once
- stiffness: float32 [16], replicated, may hold values from 0.2 to 5
- coupling: float32 [16], replicated, may hold values from 0.2 to 1
- weight_one: bfloat16 [64, 512], P('slab'), may hold values from -0.75 to 0.75
- weight_two: bfloat16 [512, 512], P('slab'), may hold values from -0.25 to 0.25
- weight_three: bfloat16 [512, 16], P('slab'), may hold values from -0.25 to 0.25
- pressure_adjoint: float32 [16, 12288], P('slab', 'date'), parts along dimension 1, may hold values from -6 to 6
- wind_adjoint: float32 [16, 12288], P('slab', 'date'), parts along dimension 1, may hold values from -6 to 6
Outputs:
- pressure_new: float32 [16, 12288], P('slab', 'date'), parts along dimension 1
- wind_new: float32 [16, 12288], P('slab', 'date'), parts along dimension 1
- pressure_grad: float32 [16, 12288], P('slab', 'date'), parts along dimension 1
- first_grad: float32 [128, 512], P(('date', 'slab')), parts along dimension 0
- second_grad: float32 [1024, 512], P(('date', 'slab')), parts along dimension 0
- third_grad: float32 [1024, 16], P(('date', 'slab')), parts along dimension 0
There are 2 independent parts, one for each index of `date`. A program takes and returns all parts, laid end to end along the dimension named above; an argument that names none is the same for every part. Nothing has to cross between parts.
Inputs may be any that keep to these rules, and one draw needn't show every extreme that they name: `neighbors`: the columns are the cells of a 8 x 768 grid stored in some order; rows 0, 1, 2, 3 give the stored positions of a column's east, west, north and south neighbours, and the column itself where the grid's edge lies on that side. `level_order`: each level appears once.
All inputs are finite; a program needn't handle non-finite values.
Results may differ from a plain program's by a relative error of at most 0.0075.
Values may be sent and summed in bfloat16 or wider, within the bound.
No kernel may reach another device: no remote copies, remote signals or barrier semaphores. Data moves between devices by JAX's collectives and lax.ppermute only.
A program may use at most 128 MiB of HBM per device.

v0:
```python
import math
import jax
import jax.numpy as jnp
from jax import lax
from jax.sharding import PartitionSpec as P


def lower_diff(field):
    return jnp.concatenate([field[1:] - field[:-1], -field[-1:]], axis=0)


def upper_diff(field):
    return jnp.concatenate([jnp.zeros_like(field[:1]), field[:-1]], axis=0) - field


def level_inverse(stiffness):
    below = jnp.concatenate([jnp.zeros((1,), jnp.float32), stiffness[:-1]])
    matrix = (
        jnp.diag(1.0 + stiffness + below)
        - jnp.diag(stiffness[:-1], 1)
        - jnp.diag(stiffness[:-1], -1)
    )
    factor = jnp.linalg.cholesky(matrix)
    identity = jnp.eye(stiffness.shape[0], dtype=jnp.float32)
    return jax.scipy.linalg.cho_solve((factor, True), identity)


def apply_inverse(inverse_matrix, rhs):
    return jnp.dot(
        inverse_matrix, rhs, precision=lax.Precision.HIGHEST, preferred_element_type=jnp.float32
    )


def contract_first(left, right):
    return lax.dot_general(
        left, right, (((0,), (0,)), ((), ())), preferred_element_type=jnp.float32
    )


def contract_last(left, right):
    return lax.dot_general(
        left, right, (((1,), (1,)), ((), ())), preferred_element_type=jnp.float32
    )


def body(
    pressure,
    density,
    vertical_wind,
    horizontal_wind,
    metric_terms,
    neighbors,
    level_order,
    stiffness,
    coupling,
    weight_one,
    weight_two,
    weight_three,
    pressure_adjoint,
    wind_adjoint,
):
    east = jnp.take(horizontal_wind[0], neighbors[0], axis=1)
    west = jnp.take(horizontal_wind[0], neighbors[1], axis=1)
    north = jnp.take(horizontal_wind[1], neighbors[2], axis=1)
    south = jnp.take(horizontal_wind[1], neighbors[3], axis=1)
    diverg = metric_terms[0] * (east - west) + metric_terms[1] * (north - south)
    star = pressure - diverg
    inverse = jnp.argsort(level_order)
    scale = 1.0 / math.sqrt(neighbors.shape[1])
    forward_raw = lax.all_to_all(
        jnp.stack([star, density, vertical_wind, diverg]).astype(jnp.bfloat16),
        "slab",
        split_axis=2,
        concat_axis=1,
        tiled=True,
    ).astype(jnp.float32)
    full_one, full_two, full_three = (
        lax.all_gather(weight_one, "slab", axis=0, tiled=True),
        lax.all_gather(weight_two, "slab", axis=0, tiled=True),
        lax.all_gather(weight_three, "slab", axis=0, tiled=True),
    )
    forward_part = jnp.take(forward_raw, inverse, axis=1)
    levels = forward_part.shape[1]
    width = forward_part.shape[2]
    couple = coupling[:, None]
    column_input = forward_part.reshape(4 * levels, width).astype(jnp.bfloat16)
    pre_one = contract_first(full_one, column_input)
    tanh_one = jnp.tanh(pre_one)
    act_one = tanh_one.astype(jnp.bfloat16)
    pre_two = contract_first(full_two, act_one)
    tanh_two = jnp.tanh(pre_two)
    act_two = tanh_two.astype(jnp.bfloat16)
    heating = contract_first(full_three, act_two)
    star_column = forward_part[0]
    rhs = forward_part[2] - couple * lower_diff(star_column) - 0.5 * forward_part[1] + heating
    inverse_matrix = level_inverse(stiffness)
    wind_next = apply_inverse(inverse_matrix, rhs)
    press_next = star_column + upper_diff(couple * wind_next)
    forward_slabs = lax.all_to_all(
        jnp.take(jnp.stack([press_next, wind_next]), level_order, axis=1).astype(jnp.bfloat16),
        "slab",
        split_axis=1,
        concat_axis=2,
        tiled=True,
    ).astype(jnp.float32)
    adjoint_raw = lax.all_to_all(
        jnp.stack([pressure_adjoint, wind_adjoint]), "slab", split_axis=2, concat_axis=1, tiled=True
    )
    adjoint_part = jnp.take(adjoint_raw, inverse, axis=1)
    wind_grad = adjoint_part[1] + couple * lower_diff(adjoint_part[0])
    rhs_grad = apply_inverse(inverse_matrix, wind_grad)
    star_grad = adjoint_part[0] - upper_diff(couple * rhs_grad)
    heat_grad = rhs_grad.astype(jnp.bfloat16)
    local_three = contract_last(act_two, heat_grad) * scale
    back_two = jnp.dot(full_three, heat_grad, preferred_element_type=jnp.float32)
    pre_two_grad = (back_two * (1.0 - tanh_two * tanh_two)).astype(jnp.bfloat16)
    local_two = contract_last(act_one, pre_two_grad) * scale
    back_one = jnp.dot(full_two, pre_two_grad, preferred_element_type=jnp.float32)
    pre_one_grad = (back_one * (1.0 - tanh_one * tanh_one)).astype(jnp.bfloat16)
    local_one = contract_last(column_input, pre_one_grad) * scale
    first_grad, second_grad, third_grad = (
        lax.psum_scatter(local_one, "slab", scatter_dimension=0, tiled=True),
        lax.psum_scatter(local_two, "slab", scatter_dimension=0, tiled=True),
        lax.psum_scatter(local_three, "slab", scatter_dimension=0, tiled=True),
    )
    input_grad = jnp.dot(full_one, pre_one_grad, preferred_element_type=jnp.float32)
    star_grad = star_grad + input_grad[:levels]
    stored_grad = jnp.take(star_grad, level_order, axis=0)
    pressure_new = forward_slabs[0]
    wind_new = forward_slabs[1]
    pressure_grad = lax.all_to_all(
        stored_grad[None].astype(jnp.bfloat16), "slab", split_axis=1, concat_axis=2, tiled=True
    ).astype(jnp.float32)[0]
    return (pressure_new, wind_new, pressure_grad, first_grad, second_grad, third_grad)


def solution(mesh):
    in_specs = (
        P("slab", "date"),
        P("slab", "date"),
        P("slab", "date"),
        P(None, "slab", "date"),
        P(),
        P(),
        P(),
        P(),
        P(),
        P("slab", None),
        P("slab", None),
        P("slab", None),
        P("slab", "date"),
        P("slab", "date"),
    )
    out_specs = (
        P("slab", "date"),
        P("slab", "date"),
        P("slab", "date"),
        P(("date", "slab"), None),
        P(("date", "slab"), None),
        P(("date", "slab"), None),
    )
    return jax.shard_map(body, mesh=mesh, in_specs=in_specs, out_specs=out_specs, check_vma=False)
```

profile of v0, /device:TPU:0, one launch (start us, length us, event | category | flops | bytes accessed | tf_op | source)
XLA Modules:
  0.0 540.4 jit_solution(8033137742579381662)
XLA Ops:
  7.2 1.2 fusion.38
  8.4 0.8 fusion.39
  9.1 34.3 %gather_fusion.4 = f32[6144]{0:T(1024)S(1)} fusion(f32[6144]{0:T(1024)S(1)} %bitcast.140, s32[6144]{0:T(1024)S(1)} %fusion.25), kind=kCustom, calls=%fused_computation.3.clone | custom fusion | bytes 73728 | tf_op jit(solution)/shard_map/jit(_take)/gather | solution.py:64
  43.5 34.3 %gather_fusion.5 = f32[6144]{0:T(1024)S(1)} fusion(f32[6144]{0:T(1024)S(1)} %bitcast.141, s32[6144]{0:T(1024)S(1)} %fusion.26), kind=kCustom, calls=%fused_computation.4.clone | custom fusion | bytes 73728 | tf_op jit(solution)/shard_map/jit(_take)/gather | solution.py:65
  77.8 34.3 %gather_fusion.2 = f32[6144]{0:T(1024)S(1)} fusion(f32[6144]{0:T(1024)S(1)} %bitcast.138, s32[6144]{0:T(1024)S(1)} %fusion.23), kind=kCustom, calls=%fused_computation.clone | custom fusion | bytes 73728 | tf_op jit(solution)/shard_map/jit(_take)/gather | solution.py:62
  112.2 34.3 %gather_fusion.3 = f32[6144]{0:T(1024)S(1)} fusion(f32[6144]{0:T(1024)S(1)} %bitcast.139, s32[6144]{0:T(1024)S(1)} %fusion.24), kind=kCustom, calls=%fused_computation.2.clone | custom fusion | bytes 73728 | tf_op jit(solution)/shard_map/jit(_take)/gather | solution.py:63
  146.9 4.0 copy.50
  151.5 34.5 %reduce.6 = bf16[6144,4]{1,0:T(8,128)(2,1)} reduce(bf16[6144,1,4]{2,1,0:T(2,128)(2,1)S(1)} %bitcast.142, bf16[]{:T(256)} %broadcast.246), dimensions={1}, to_apply=%bitcast.107.reduce_sub_computation | reduce | bytes 98306
  186.0 4.4 reshape.350
  190.4 7.4 %all-to-all-start = ((bf16[16,2,768]{2,1,0:T(2,128)(2,1)}), bf16[16,2,768]{2,1,0:T(2,128)(2,1)S(1)}, u32[]{:S(2)}, u32[]{:S(2)}) async-start(bf16[16,2,768]{2,1,0:T(2,128)(2,1)} %reshape.350), calls=%async_computation | async-start | bytes 98304 | tf_op jit(solution)/shard_map/all_to_all | solution.py:70
  197.8 1.2 sort.17
  199.2 21.9 %all-gather = bf16[16,4,512]{2,1,0:T(4,128)(2,1)S(1)} all-gather(bf16[1,4,512]{2,1,0:T(4,128)(2,1)S(1)} %bitcast.168), channel_id=1, replica_groups=mesh['date'=2,'slab'=16] {'slab'}, dimensions={0}, use_global_device_ids=true | all-gather | bytes 69632 | tf_op jit(solution)/shard_map/all_gather | solution.py:78
  221.1 20.3 %all_gather.10 = bf16[512,512]{1,0:T(8,128)(2,1)} all-gather(bf16[32,512]{1,0:T(8,128)(2,1)S(1)} %copy-done.2), channel_id=1, replica_groups=mesh['date'=2,'slab'=16] {'slab'}, dimensions={0}, use_global_device_ids=true | all-gather | bytes 557056 | tf_op jit(solution)/shard_map/all_gather | solution.py:79
  241.4 19.3 %all-gather.1 = bf16[16,32,16]{1,2,0:T(8,128)(2,1)S(1)} all-gather(bf16[1,32,16]{1,2,0:T(8,128)(2,1)S(1)} %bitcast.169), channel_id=1, replica_groups=mesh['date'=2,'slab'=16] {'slab'}, dimensions={0}, use_global_device_ids=true | all-gather | bytes 17408 | tf_op jit(solution)/shard_map/all_gather | solution.py:80
  261.0 1.4 cholesky.17
  262.5 0.6 compare_reduce_fusion
  263.1 0.6 fusion.28
  263.8 1.2 custom-call.10
  265.4 3.3 copy.56
  269.2 28.4 %reduce.7 = f32[6144,2]{1,0:T(8,128)} reduce(f32[6144,1,2]{2,1,0:T(1,128)S(1)} %bitcast.143, f32[]{:T(128)} %broadcast.247), dimensions={1}, to_apply=%bitcast.109.reduce_sub_computation | reduce | bytes 98308
  297.6 4.3 reshape.352
  302.0 3.5 all-to-all-start.2
  305.7 4.0 reshape.351
  309.7 2.9 copy.51
  312.7 0.6 gather_fusion
  313.4 0.8 reduce.8
  314.2 4.5 reshape.353
  318.7 1.2 copy.58
  319.9 0.6 gather_fusion.7
  321.0 1.4 convolution_tanh_fusion
  323.6 0.8 copy.63
  324.9 0.8 convolution_multiply_fusion.3
  325.8 1.4 convolution_multiply_fusion
  328.3 0.7 reduce.9
  329.0 0.7 reshape.354
  329.7 6.0 %all-to-all-start.3 = ((bf16[16,2,192]{2,1,0:T(2,128)(2,1)}), bf16[16,2,192]{2,1,0:T(2,128)(2,1)S(1)}, u32[]{:S(2)}, u32[]{:S(2)}) async-start(bf16[16,2,192]{2,1,0:T(2,128)(2,1)} %reshape.354), calls=%async_computation.3 | async-start | bytes 32768 | tf_op jit(solution)/shard_map/all_to_all | solution.py:131
  335.7 0.6 gather_fusion.6
  336.3 0.7 bitcast_convert_fusion
  337.0 5.1 all-to-all-done.3
  342.2 3.5 all-to-all-start.1
  347.0 0.6 convert.31
  347.7 4.5 all-to-all-done.1
  352.2 0.7 fusion.40
  352.8 28.3 %reduce-scatter.7.cloned.1.call-done = f32[32,16]{1,0:T(8,128)} async-done(((f32[512,16]{1,0:T(8,128)}), f32[32,16]{1,0:T(8,128)}) %reduce-scatter.7.cloned.1.call-update) | async-done | bytes 2064
  381.1 1.4 copy.64
  382.5 88.1 %all-reduce.6.cloned.1.call-done = f32[64,512]{1,0:T(8,128)} async-done(((f32[64,512]{1,0:T(8,128)}), f32[64,512]{1,0:T(8,128)}) %all-reduce.6.cloned.1.call-update) | async-done | bytes 131088
  470.6 1.3 constant_dynamic-slice_fusion
  472.0 61.9 %reduce-scatter.5.cloned.1.call-done = f32[32,512]{1,0:T(8,128)} async-done(((f32[512,512]{1,0:T(8,128)}), f32[32,512]{1,0:T(8,128)}) %reduce-scatter.5.cloned.1.call-update) | async-done | bytes 65552 | tf_op jit(solution)/shard_map/reduce_scatter | solution.py:123
  (97 shorter events, 6.6 us)
Async XLA Ops:
  112.1 34.4 %copy-start.4 = (f32[1,6144]{1,0:T(1,128)S(1)}, f32[1,6144]{1,0:T(1,128)}, u32[]{:S(2)}) copy-start(f32[1,6144]{1,0:T(1,128)} %param.19) | copy-start | bytes 73732
  112.1 34.4 %copy-start.1 = (f32[2,6144]{1,0:T(2,128)S(1)}, f32[2,6144]{1,0:T(2,128)}, u32[]{:S(2)}) copy-start(f32[2,6144]{1,0:T(2,128)} %param.22) | copy-start | bytes 147460
  112.1 34.4 %copy-start.3 = (f32[1,6144]{1,0:T(1,128)S(1)}, f32[1,6144]{1,0:T(1,128)}, u32[]{:S(2)}) copy-start(f32[1,6144]{1,0:T(1,128)} %param.18) | copy-start | bytes 73732
  112.1 34.5 %copy-start.5 = (f32[1,6144]{1,0:T(1,128)S(1)}, f32[1,6144]{1,0:T(1,128)}, u32[]{:S(2)}) copy-start(f32[1,6144]{1,0:T(1,128)} %param.20) | copy-start | bytes 73732
  151.4 46.3 %copy-start.13 = (s32[16]{0:T(128)S(1)}, s32[16]{0:T(128)}, u32[]{:S(2)}) copy-start(s32[16]{0:T(128)} %param.24) | copy-start | bytes 196
  151.5 47.7 %copy-start.8 = (bf16[4,512]{1,0:T(4,128)(2,1)S(1)}, bf16[4,512]{1,0:T(4,128)(2,1)}, u32[]{:S(2)}) copy-start(bf16[4,512]{1,0:T(4,128)(2,1)} %param.27) | copy-start | bytes 12292
  151.5 69.6 %copy-start.2 = (bf16[32,512]{1,0:T(8,128)(2,1)S(1)}, bf16[32,512]{1,0:T(8,128)(2,1)}, u32[]{:S(2)}) copy-start(bf16[32,512]{1,0:T(8,128)(2,1)} %param.28) | copy-start | bytes 98308
  151.5 89.9 %copy-start.9 = (bf16[32,16]{0,1:T(8,128)(2,1)S(1)}, bf16[32,16]{0,1:T(8,128)(2,1)}, u32[]{:S(2)}) copy-start(bf16[32,16]{0,1:T(8,128)(2,1)} %param.29) | copy-start | bytes 3076
  151.5 109.3 %copy-start.10 = (f32[16]{0:T(128)S(1)}, f32[16]{0:T(128)}, u32[]{:S(2)}) copy-start(f32[16]{0:T(128)} %param.25) | copy-start | bytes 196
  151.5 109.3 %copy-start.12 = (pred[16]{0:T(512)(128)(4,1)S(1)}, pred[16]{0:T(512)(128)(4,1)}, u32[]{:S(2)}) copy-start(pred[16]{0:T(512)(128)(4,1)} %constant.116.clone.1) | copy-start | bytes 52
  151.5 113.9 %copy-start.6 = (f32[1,6144]{1,0:T(1,128)S(1)}, f32[1,6144]{1,0:T(1,128)}, u32[]{:S(2)}) copy-start(f32[1,6144]{1,0:T(1,128)} %param.31) | copy-start | bytes 73732
  151.5 113.9 %copy-start.7 = (f32[1,6144]{1,0:T(1,128)S(1)}, f32[1,6144]{1,0:T(1,128)}, u32[]{:S(2)}) copy-start(f32[1,6144]{1,0:T(1,128)} %param.30) | copy-start | bytes 73732
  190.4 111.6 %all-to-all-start = ((bf16[16,2,768]{2,1,0:T(2,128)(2,1)}), bf16[16,2,768]{2,1,0:T(2,128)(2,1)S(1)}, u32[]{:S(2)}, u32[]{:S(2)}) async-start(bf16[16,2,768]{2,1,0:T(2,128)(2,1)} %reshape.350), calls=%async_computation | async-start | bytes 98304 | tf_op jit(solution)/shard_map/all_to_all | solution.py:70
  302.0 11.4 %all-to-all-start.2 = ((f32[16,1,768]{2,1,0:T(1,128)}), f32[16,1,768]{2,1,0:T(1,128)S(1)}, u32[]{:S(2)}, u32[]{:S(2)}) async-start(f32[16,1,768]{2,1,0:T(1,128)} %reshape.352), calls=%async_computation.2 | async-start | bytes 98304 | tf_op jit(solution)/shard_map/all_to_all | solution.py:106
  305.5 75.7 %reduce-scatter.7.cloned.1.call-start = ((), (), s32[]{:S(2)}) async-start(), calls=%async_computation.7 | async-start | bytes 278528
  318.7 3.7 copy-start.11
  320.7 3.8 copy-start
  324.4 146.2 %all-reduce.6.cloned.1.call-start = ((), (), s32[]{:S(2)}) async-start(), calls=%async_computation.8 | async-start | bytes 262144
  324.9 20.8 %copy-start.14 = (u32[32]{0:T(128)S(1)}, u32[32]{0:T(128)}, u32[]{:S(2)}) copy-start(u32[32]{0:T(128)} %constant.136) | copy-start | bytes 388
  325.8 208.2 %reduce-scatter.5.cloned.1.call-start = ((), (), s32[]{:S(2)}) async-start(), calls=%async_computation.6 | async-start | bytes 1114112 | tf_op jit(solution)/shard_map/reduce_scatter | solution.py:123
  329.7 12.5 %all-to-all-start.3 = ((bf16[16,2,192]{2,1,0:T(2,128)(2,1)}), bf16[16,2,192]{2,1,0:T(2,128)(2,1)S(1)}, u32[]{:S(2)}, u32[]{:S(2)}) async-start(bf16[16,2,192]{2,1,0:T(2,128)(2,1)} %reshape.354), calls=%async_computation.3 | async-start | bytes 32768 | tf_op jit(solution)/shard_map/all_to_all | solution.py:131
  342.2 10.0 %all-to-all-start.1 = ((bf16[2,16,384]{2,0,1:T(2,128)(2,1)}), bf16[2,16,384]{2,0,1:T(2,128)(2,1)S(1)}, u32[]{:S(2)}, u32[]{:S(2)}) async-start(bf16[2,16,384]{2,0,1:T(2,128)(2,1)} %bitcast_convert_fusion), calls=%async_computation.1 | async-start | bytes 49152 | tf_op jit(solution)/shard_map/all_to_all | solution.py:99
Sparse Core Ops, SparseCore 0:
  324.5 56.5 reduce-scatter.6
  384.6 86.0 all-reduce.5
  474.8 59.0 reduce-scatter.4
where the time goes:
time: 541 us; the launch traced here: 540 us
  waiting for transfers between devices  188 us (35%)
  local copies, waits for them, and re-layouts  177 us (33%)
  other arithmetic  72 us (13%)
  blocking collectives  61.4 us (11%)
  starting transfers between devices  20.7 us (4%)
  between operations  15 us (3%)
  matrix products  6.09 us (1%)
    unnamed x5, waiting for transfers between devices  116 us
    unnamed x3, other arithmetic  63.6 us
    reduce_scatter x1, waiting for transfers between devices, body(): lax.psum_scatter(local_two, 'slab', scatter_dimension=0, tiled=True)  61.9 us
    gather x1, local copies, waits for them, and re-layouts, body(): south = jnp.take(horizontal_wind[1], neighbors[3], axis=1)  34.3 us
    gather x1, local copies, waits for them, and re-layouts, body(): east = jnp.take(horizontal_wind[0], neighbors[0], axis=1)  34.3 us
    gather x1, local copies, waits for them, and re-layouts, body(): west = jnp.take(horizontal_wind[0], neighbors[1], axis=1)  34.3 us
    gather x1, local copies, waits for them, and re-layouts, body(): north = jnp.take(horizontal_wind[1], neighbors[2], axis=1)  34.3 us
    unnamed x44, local copies, waits for them, and re-layouts  23.4 us
  transfers between devices with their start and end apart: 7, of which 5 were waited for; matrix products, arithmetic and copies ran while one was open for 11% of the time, Pallas kernels for 0%

commit v1 on v0

--- a/solution.py
+++ b/solution.py
@@ -3,6 +3,29 @@
 import jax.numpy as jnp
 from jax import lax
 from jax.sharding import PartitionSpec as P
+
+
+def process_the_sides(array_here, axis_key):
+    fresh, y_new, after = (lax.axis_size(axis_key), lax.axis_index(axis_key), array_here.shape[0])
+    xs_all = tuple(((ii, (ii + 1) % fresh) for ii in range(fresh)))
+    series = tuple(((ii, (ii - 1) % fresh) for ii in range(fresh)))
+    outer = jnp.zeros(
+        (*array_here.shape[:0], fresh * after, *array_here.shape[1:]), array_here.dtype
+    )
+    outer = lax.dynamic_update_slice_in_dim(outer, array_here, y_new * after, axis=0)
+    item_now = clean = array_here
+    z2 = fresh // 2
+    for ix in range(1, z2 + 1):
+        item_now = lax.ppermute(item_now, axis_key, xs_all)
+        outer = lax.dynamic_update_slice_in_dim(
+            outer, item_now, (y_new - ix) % fresh * after, axis=0
+        )
+        if ix < fresh - z2:
+            clean = lax.ppermute(clean, axis_key, series)
+            outer = lax.dynamic_update_slice_in_dim(
+                outer, clean, (y_new + ix) % fresh * after, axis=0
+            )
+    return outer
 
 
 def lower_diff(field):
@@ -76,7 +99,7 @@
     ).astype(jnp.float32)
     full_one, full_two, full_three = (
         lax.all_gather(weight_one, "slab", axis=0, tiled=True),
-        lax.all_gather(weight_two, "slab", axis=0, tiled=True),
+        process_the_sides(weight_two, "slab"),
         lax.all_gather(weight_three, "slab", axis=0, tiled=True),
     )
     forward_part = jnp.take(forward_raw, inverse, axis=1)

time: 541 us -> 565 us (1.044)
  starting transfers between devices: 20.7 us -> 46.8 us
  blocking collectives: 61.4 us -> 39.1 us
  local copies, waits for them, and re-layouts: 177 us -> 190 us
    ppermute x0 -> x15, starting transfers between devices: none -> 32.2 us  [the longest x7 31.1 us: process_the_sides(): clean = lax.ppermute(clean, axis_key, series)]
    all_gather x1 -> x0, blocking collectives: 20.3 us -> none  [body(): lax.all_gather(weight_two, 'slab', axis=0, tiled=True)]
    dynamic_update_slice x0 -> x16, local copies, waits for them, and re-layouts: none -> 11.9 us  [the longest x8 6.35 us: process_the_sides(): lax.dynamic_update_slice_in_dim(outer, item_now, (y_new - ix) % fresh * a...]
    ppermute x0 -> x15, waiting for transfers between devices: none -> 6.5 us  [the longest x8 6.48 us: process_the_sides(): item_now = lax.ppermute(item_now, axis_key, xs_all)]
    unnamed x44 -> x46, local copies, waits for them, and re-layouts: 23.4 us -> 23.4 us
  transfers between devices with their start and end apart: 7 -> 22, of which waited for: 5 -> 10; matrix products, arithmetic and copies ran while one was open for 11% -> 47% of each run, Pallas kernels for 0% -> 0%
where the time goes in v1:
time: 565 us; the launch traced here: 564 us
  waiting for transfers between devices  192 us (34%)
  local copies, waits for them, and re-layouts  190 us (34%)
  other arithmetic  72.5 us (13%)
  starting transfers between devices  46.8 us (8%)
  blocking collectives  39.1 us (7%)
  between operations  15.3 us (3%)
  matrix products  7.3 us (1%)
    unnamed x5, waiting for transfers between devices  114 us
    unnamed x3, other arithmetic  63.6 us
    reduce_scatter x1, waiting for transfers between devices, body(): lax.psum_scatter(local_two, 'slab', scatter_dimension=0, tiled=True)  61.9 us
    gather x1, local copies, waits for them, and re-layouts, body(): south = jnp.take(horizontal_wind[1], neighbors[3], axis=1)  34.3 us
    gather x1, local copies, waits for them, and re-layouts, body(): east = jnp.take(horizontal_wind[0], neighbors[0], axis=1)  34.3 us
    gather x1, local copies, waits for them, and re-layouts, body(): west = jnp.take(horizontal_wind[0], neighbors[1], axis=1)  34.3 us
    gather x1, local copies, waits for them, and re-layouts, body(): north = jnp.take(horizontal_wind[1], neighbors[2], axis=1)  34.3 us
    ppermute x7, starting transfers between devices, process_the_sides(): clean = lax.ppermute(clean, axis_key, series)  31.1 us
  transfers between devices with their start and end apart: 22, of which 10 were waited for; matrix products, arithmetic and copies ran while one was open for 47% of the time, Pallas kernels for 0%

profile of v1, /device:TPU:0, one launch (start us, length us, event | category | flops | bytes accessed | tf_op | source)
XLA Modules:
  0.0 563.7 jit_solution(7772306475349371403)
XLA Ops:
  7.7 5.0 collective-permute-start.1
  12.7 1.2 fusion.39
  14.7 34.3 %gather_fusion.4 = f32[6144]{0:T(1024)S(1)} fusion(f32[6144]{0:T(1024)S(1)} %bitcast.146, s32[6144]{0:T(1024)S(1)} %fusion.24), kind=kCustom, calls=%fused_computation.3.clone | custom fusion | bytes 73728 | tf_op jit(solution)/shard_map/jit(_take)/gather | solution.py:87
  49.0 34.3 %gather_fusion.5 = f32[6144]{0:T(1024)S(1)} fusion(f32[6144]{0:T(1024)S(1)} %bitcast.147, s32[6144]{0:T(1024)S(1)} %fusion.25), kind=kCustom, calls=%fused_computation.4.clone | custom fusion | bytes 73728 | tf_op jit(solution)/shard_map/jit(_take)/gather | solution.py:88
  83.3 34.3 %gather_fusion.2 = f32[6144]{0:T(1024)S(1)} fusion(f32[6144]{0:T(1024)S(1)} %bitcast.144, s32[6144]{0:T(1024)S(1)} %fusion.22), kind=kCustom, calls=%fused_computation.clone | custom fusion | bytes 73728 | tf_op jit(solution)/shard_map/jit(_take)/gather | solution.py:85
  117.7 34.3 %gather_fusion.3 = f32[6144]{0:T(1024)S(1)} fusion(f32[6144]{0:T(1024)S(1)} %bitcast.145, s32[6144]{0:T(1024)S(1)} %fusion.23), kind=kCustom, calls=%fused_computation.2.clone | custom fusion | bytes 73728 | tf_op jit(solution)/shard_map/jit(_take)/gather | solution.py:86
  152.4 4.0 copy.60
  157.0 34.5 %reduce.6 = bf16[6144,4]{1,0:T(8,128)(2,1)} reduce(bf16[6144,1,4]{2,1,0:T(2,128)(2,1)S(1)} %bitcast.148, bf16[]{:T(256)} %broadcast.263), dimensions={1}, to_apply=%bitcast.113.reduce_sub_computation | reduce | bytes 98306
  191.6 4.4 reshape.350
  195.9 3.7 all-to-all-start
  199.9 1.2 sort.17
  202.5 1.4 cholesky.17
  205.3 1.2 custom-call.10
  206.9 0.8 broadcast_in_dim.113
  208.4 21.5 %all-gather = bf16[16,4,512]{2,1,0:T(4,128)(2,1)S(1)} all-gather(bf16[1,4,512]{2,1,0:T(4,128)(2,1)S(1)} %bitcast.174), channel_id=1, replica_groups=mesh['date'=2,'slab'=16] {'slab'}, dimensions={0}, use_global_device_ids=true | all-gather | bytes 69632 | tf_op jit(solution)/shard_map/all_gather | solution.py:101
  229.9 17.6 %all-gather.1 = bf16[16,32,16]{1,2,0:T(8,128)(2,1)S(1)} all-gather(bf16[1,32,16]{1,2,0:T(8,128)(2,1)S(1)} %bitcast.175), channel_id=1, replica_groups=mesh['date'=2,'slab'=16] {'slab'}, dimensions={0}, use_global_device_ids=true | all-gather | bytes 17408 | tf_op jit(solution)/shard_map/all_gather | solution.py:103
  247.7 3.3 copy.66
  251.5 28.4 %reduce.7 = f32[6144,2]{1,0:T(8,128)} reduce(f32[6144,1,2]{2,1,0:T(1,128)S(1)} %bitcast.149, f32[]{:T(128)} %broadcast.264), dimensions={1}, to_apply=%bitcast.115.reduce_sub_computation | reduce | bytes 98308
  279.9 4.3 reshape.352
  284.6 4.1 collective-permute-start.3
  290.4 4.4 collective-permute-start.5
  294.8 1.4 constant_dynamic-update-slice_fusion.12
  296.8 3.5 all-to-all-start.2
  300.5 4.0 reshape.351
  304.5 2.9 copy.61
  309.0 4.5 reshape.353
  313.6 1.2 copy.68
  316.2 4.2 collective-permute-start.7
  320.4 1.4 constant_dynamic-update-slice_fusion.10
  321.7 1.4 constant_dynamic-update-slice_fusion.9
  323.1 4.4 collective-permute-start.9
  329.2 4.4 collective-permute-start.11
  335.2 4.4 collective-permute-start.13
  342.4 4.8 collective-permute-done.14
  347.9 1.5 convolution_tanh_fusion
  350.5 0.8 copy.77
  351.5 1.5 fusion
  352.9 0.8 convolution_multiply_fusion.2
  353.8 1.5 convolution_multiply_fusion
  357.8 3.5 all-to-all-start.3
  362.6 5.1 all-to-all-done.3
  367.7 3.5 all-to-all-start.1
  373.2 4.5 all-to-all-done.1
  378.4 26.0 %reduce-scatter.7.cloned.1.call-done = f32[32,16]{1,0:T(8,128)} async-done(((f32[512,16]{1,0:T(8,128)}), f32[32,16]{1,0:T(8,128)}) %reduce-scatter.7.cloned.1.call-update) | async-done | bytes 2064
  404.4 1.4 copy.78
  405.8 88.1 %all-reduce.6.cloned.1.call-done = f32[64,512]{1,0:T(8,128)} async-done(((f32[64,512]{1,0:T(8,128)}), f32[64,512]{1,0:T(8,128)}) %all-reduce.6.cloned.1.call-update) | async-done | bytes 131088
  493.9 1.3 constant_dynamic-slice_fusion
  495.2 61.9 %reduce-scatter.5.cloned.1.call-done = f32[32,512]{1,0:T(8,128)} async-done(((f32[512,512]{1,0:T(8,128)}), f32[32,512]{1,0:T(8,128)}) %reduce-scatter.5.cloned.1.call-update) | async-done | bytes 65552 | tf_op jit(solution)/shard_map/reduce_scatter | solution.py:146
  (145 shorter events, 26.0 us)
Async XLA Ops:
  7.2 277.0 %collective-permute-start = (bf16[32,512]{1,0:T(8,128)(2,1)}, bf16[32,512]{1,0:T(8,128)(2,1)S(1)}, u32[]{:S(2)}, u32[]{:S(2)}) collective-permute-start(bf16[32,512]{1,0:T(8,128)(2,1)} %param.28), channel_id=1, source_target_pairs={{0,1},{1,2},{2,3},{3,4},{4,5},{5,6},{6,7},{7,8},{8,9},{9,10},{10,1... | collective-permute-start | bytes 98312 | tf_op jit(solution)/shard_map/ppermute | solution.py:19
  7.7 276.9 %collective-permute-start.1 = (bf16[32,512]{1,0:T(8,128)(2,1)}, bf16[32,512]{1,0:T(8,128)(2,1)S(1)}, u32[]{:S(2)}, u32[]{:S(2)}) collective-permute-start(bf16[32,512]{1,0:T(8,128)(2,1)} %param.28), channel_id=1, source_target_pairs={{0,15},{1,0},{2,1},{3,2},{4,3},{5,4},{6,5},{7,6},{8,7},{9,8},{10,9... | collective-permute-start | bytes 98312 | tf_op jit(solution)/shard_map/ppermute | solution.py:24
  117.6 34.4 %copy-start.3 = (f32[1,6144]{1,0:T(1,128)S(1)}, f32[1,6144]{1,0:T(1,128)}, u32[]{:S(2)}) copy-start(f32[1,6144]{1,0:T(1,128)} %param.19) | copy-start | bytes 73732
  117.7 34.4 %copy-start = (f32[2,6144]{1,0:T(2,128)S(1)}, f32[2,6144]{1,0:T(2,128)}, u32[]{:S(2)}) copy-start(f32[2,6144]{1,0:T(2,128)} %param.22) | copy-start | bytes 147460
  117.7 34.4 %copy-start.2 = (f32[1,6144]{1,0:T(1,128)S(1)}, f32[1,6144]{1,0:T(1,128)}, u32[]{:S(2)}) copy-start(f32[1,6144]{1,0:T(1,128)} %param.18) | copy-start | bytes 73732
  117.7 34.5 %copy-start.4 = (f32[1,6144]{1,0:T(1,128)S(1)}, f32[1,6144]{1,0:T(1,128)}, u32[]{:S(2)}) copy-start(f32[1,6144]{1,0:T(1,128)} %param.20) | copy-start | bytes 73732
  157.0 43.0 %copy-start.14 = (s32[16]{0:T(128)S(1)}, s32[16]{0:T(128)}, u32[]{:S(2)}) copy-start(s32[16]{0:T(128)} %param.24) | copy-start | bytes 196
  157.0 45.4 %copy-start.10 = (f32[16]{0:T(128)S(1)}, f32[16]{0:T(128)}, u32[]{:S(2)}) copy-start(f32[16]{0:T(128)} %param.25) | copy-start | bytes 196
  157.0 45.4 %copy-start.13 = (pred[16]{0:T(512)(128)(4,1)S(1)}, pred[16]{0:T(512)(128)(4,1)}, u32[]{:S(2)}) copy-start(pred[16]{0:T(512)(128)(4,1)} %constant.205.clone.1) | copy-start | bytes 52
  157.0 50.7 %copy-start.1 = (bf16[32,512]{1,0:T(8,128)(2,1)S(1)}, bf16[32,512]{1,0:T(8,128)(2,1)}, u32[]{:S(2)}) copy-start(bf16[32,512]{1,0:T(8,128)(2,1)} %param.28) | copy-start | bytes 98308
  157.0 51.3 %copy-start.5 = (f32[1,6144]{1,0:T(1,128)S(1)}, f32[1,6144]{1,0:T(1,128)}, u32[]{:S(2)}) copy-start(f32[1,6144]{1,0:T(1,128)} %param.31) | copy-start | bytes 73732
  157.0 51.3 %copy-start.6 = (f32[1,6144]{1,0:T(1,128)S(1)}, f32[1,6144]{1,0:T(1,128)}, u32[]{:S(2)}) copy-start(f32[1,6144]{1,0:T(1,128)} %param.30) | copy-start | bytes 73732
  157.0 51.4 %copy-start.7 = (bf16[4,512]{1,0:T(4,128)(2,1)S(1)}, bf16[4,512]{1,0:T(4,128)(2,1)}, u32[]{:S(2)}) copy-start(bf16[4,512]{1,0:T(4,128)(2,1)} %param.27) | copy-start | bytes 12292
  157.0 72.9 %copy-start.8 = (bf16[32,16]{0,1:T(8,128)(2,1)S(1)}, bf16[32,16]{0,1:T(8,128)(2,1)}, u32[]{:S(2)}) copy-start(bf16[32,16]{0,1:T(8,128)(2,1)} %param.29) | copy-start | bytes 3076
  195.9 100.8 %all-to-all-start = ((bf16[16,2,768]{2,1,0:T(2,128)(2,1)}), bf16[16,2,768]{2,1,0:T(2,128)(2,1)S(1)}, u32[]{:S(2)}, u32[]{:S(2)}) async-start(bf16[16,2,768]{2,1,0:T(2,128)(2,1)} %reshape.350), calls=%async_computation | async-start | bytes 98304 | tf_op jit(solution)/shard_map/all_to_all | solution.py:93
  284.2 6.1 %collective-permute-start.2 = (bf16[32,512]{1,0:T(8,128)(2,1)S(1)}, bf16[32,512]{1,0:T(8,128)(2,1)}, u32[]{:S(2)}, u32[]{:S(2)}) collective-permute-start(bf16[32,512]{1,0:T(8,128)(2,1)S(1)} %collective-permute-done), channel_id=1, source_target_pairs={{0,1},{1,2},{2,3},{3,4},{4,5},{5,6},{6,7},{7,8},{8,9},{9,10},{10,1... | collective-permute-start | bytes 98312 | tf_op jit(solution)/shard_map/ppermute | solution.py:19
  284.6 5.8 %collective-permute-start.3 = (bf16[32,512]{1,0:T(8,128)(2,1)S(1)}, bf16[32,512]{1,0:T(8,128)(2,1)S(1)}, u32[]{:S(2)}, u32[]{:S(2)}) collective-permute-start(bf16[32,512]{1,0:T(8,128)(2,1)S(1)} %collective-permute-done.1), channel_id=1, source_target_pairs={{0,15},{1,0},{2,1},{3,2},{4,3},{5,4},{6,5},{7,6},{8,7},{9,8},{10,9... | collective-permute-start | bytes 98312 | tf_op jit(solution)/shard_map/ppermute | solution.py:24
  290.4 25.5 %collective-permute-start.4 = (bf16[32,512]{1,0:T(8,128)(2,1)}, bf16[32,512]{1,0:T(8,128)(2,1)}, u32[]{:S(2)}, u32[]{:S(2)}) collective-permute-start(bf16[32,512]{1,0:T(8,128)(2,1)} %collective-permute-done.2), channel_id=1, source_target_pairs={{0,1},{1,2},{2,3},{3,4},{4,5},{5,6},{6,7},{7,8},{8,9},{9,10},{10,1... | collective-permute-start | bytes 98312 | tf_op jit(solution)/shard_map/ppermute | solution.py:19
  290.4 25.8 %collective-permute-start.5 = (bf16[32,512]{1,0:T(8,128)(2,1)S(1)}, bf16[32,512]{1,0:T(8,128)(2,1)}, u32[]{:S(2)}, u32[]{:S(2)}) collective-permute-start(bf16[32,512]{1,0:T(8,128)(2,1)S(1)} %collective-permute-done.3), channel_id=1, source_target_pairs={{0,15},{1,0},{2,1},{3,2},{4,3},{5,4},{6,5},{7,6},{8,7},{9,8},{10,9... | collective-permute-start | bytes 98312 | tf_op jit(solution)/shard_map/ppermute | solution.py:24
  296.8 11.4 %all-to-all-start.2 = ((f32[16,1,768]{2,1,0:T(1,128)}), f32[16,1,768]{2,1,0:T(1,128)S(1)}, u32[]{:S(2)}, u32[]{:S(2)}) async-start(f32[16,1,768]{2,1,0:T(1,128)} %reshape.352), calls=%async_computation.2 | async-start | bytes 98304 | tf_op jit(solution)/shard_map/all_to_all | solution.py:129
  300.3 104.1 %reduce-scatter.7.cloned.1.call-start = ((), (), s32[]{:S(2)}) async-start(), calls=%async_computation.7 | async-start | bytes 278528
  313.5 1.9 copy-start.12
  313.5 35.8 %copy-start.11 = (f32[16]{0:T(128)S(1)}, f32[16]{0:T(128)}, u32[]{:S(2)}) copy-start(f32[16]{0:T(128)} %param.26) | copy-start | bytes 196
  315.9 7.2 %collective-permute-start.6 = (bf16[32,512]{1,0:T(8,128)(2,1)}, bf16[32,512]{1,0:T(8,128)(2,1)S(1)}, u32[]{:S(2)}, u32[]{:S(2)}) collective-permute-start(bf16[32,512]{1,0:T(8,128)(2,1)} %collective-permute-done.4), channel_id=1, source_target_pairs={{0,1},{1,2},{2,3},{3,4},{4,5},{5,6},{6,7},{7,8},{8,9},{9,10},{10,1... | collective-permute-start | bytes 98312 | tf_op jit(solution)/shard_map/ppermute | solution.py:19
  316.2 6.9 %collective-permute-start.7 = (bf16[32,512]{1,0:T(8,128)(2,1)}, bf16[32,512]{1,0:T(8,128)(2,1)S(1)}, u32[]{:S(2)}, u32[]{:S(2)}) collective-permute-start(bf16[32,512]{1,0:T(8,128)(2,1)} %collective-permute-done.5), channel_id=1, source_target_pairs={{0,15},{1,0},{2,1},{3,2},{4,3},{5,4},{6,5},{7,6},{8,7},{9,8},{10,9... | collective-permute-start | bytes 98312 | tf_op jit(solution)/shard_map/ppermute | solution.py:24
  323.1 6.1 %collective-permute-start.8 = (bf16[32,512]{1,0:T(8,128)(2,1)S(1)}, bf16[32,512]{1,0:T(8,128)(2,1)S(1)}, u32[]{:S(2)}, u32[]{:S(2)}) collective-permute-start(bf16[32,512]{1,0:T(8,128)(2,1)S(1)} %collective-permute-done.6), channel_id=1, source_target_pairs={{0,1},{1,2},{2,3},{3,4},{4,5},{5,6},{6,7},{7,8},{8,9},{9,10},{10,1... | collective-permute-start | bytes 98312 | tf_op jit(solution)/shard_map/ppermute | solution.py:19
  323.1 6.1 %collective-permute-start.9 = (bf16[32,512]{1,0:T(8,128)(2,1)S(1)}, bf16[32,512]{1,0:T(8,128)(2,1)S(1)}, u32[]{:S(2)}, u32[]{:S(2)}) collective-permute-start(bf16[32,512]{1,0:T(8,128)(2,1)S(1)} %collective-permute-done.7), channel_id=1, source_target_pairs={{0,15},{1,0},{2,1},{3,2},{4,3},{5,4},{6,5},{7,6},{8,7},{9,8},{10,9... | collective-permute-start | bytes 98312 | tf_op jit(solution)/shard_map/ppermute | solution.py:24
  329.1 6.0 %collective-permute-start.10 = (bf16[32,512]{1,0:T(8,128)(2,1)S(1)}, bf16[32,512]{1,0:T(8,128)(2,1)S(1)}, u32[]{:S(2)}, u32[]{:S(2)}) collective-permute-start(bf16[32,512]{1,0:T(8,128)(2,1)S(1)} %collective-permute-done.8), channel_id=1, source_target_pairs={{0,1},{1,2},{2,3},{3,4},{4,5},{5,6},{6,7},{7,8},{8,9},{9,10},{10,1... | collective-permute-start | bytes 98312 | tf_op jit(solution)/shard_map/ppermute | solution.py:19
  329.2 6.0 %collective-permute-start.11 = (bf16[32,512]{1,0:T(8,128)(2,1)S(1)}, bf16[32,512]{1,0:T(8,128)(2,1)S(1)}, u32[]{:S(2)}, u32[]{:S(2)}) collective-permute-start(bf16[32,512]{1,0:T(8,128)(2,1)S(1)} %collective-permute-done.9), channel_id=1, source_target_pairs={{0,15},{1,0},{2,1},{3,2},{4,3},{5,4},{6,5},{7,6},{8,7},{9,8},{10,9... | collective-permute-start | bytes 98312 | tf_op jit(solution)/shard_map/ppermute | solution.py:24
  335.2 6.0 %collective-permute-start.12 = (bf16[32,512]{1,0:T(8,128)(2,1)S(1)}, bf16[32,512]{1,0:T(8,128)(2,1)S(1)}, u32[]{:S(2)}, u32[]{:S(2)}) collective-permute-start(bf16[32,512]{1,0:T(8,128)(2,1)S(1)} %collective-permute-done.10), channel_id=1, source_target_pairs={{0,1},{1,2},{2,3},{3,4},{4,5},{5,6},{6,7},{7,8},{8,9},{9,10},{10,1... | collective-permute-start | bytes 98312 | tf_op jit(solution)/shard_map/ppermute | solution.py:19
  335.2 6.6 %collective-permute-start.13 = (bf16[32,512]{1,0:T(8,128)(2,1)S(1)}, bf16[32,512]{1,0:T(8,128)(2,1)S(1)}, u32[]{:S(2)}, u32[]{:S(2)}) collective-permute-start(bf16[32,512]{1,0:T(8,128)(2,1)S(1)} %collective-permute-done.11), channel_id=1, source_target_pairs={{0,15},{1,0},{2,1},{3,2},{4,3},{5,4},{6,5},{7,6},{8,7},{9,8},{10,9... | collective-permute-start | bytes 98312 | tf_op jit(solution)/shard_map/ppermute | solution.py:24
  341.2 6.0 %collective-permute-start.14 = (bf16[32,512]{1,0:T(8,128)(2,1)S(1)}, bf16[32,512]{1,0:T(8,128)(2,1)S(1)}, u32[]{:S(2)}, u32[]{:S(2)}) collective-permute-start(bf16[32,512]{1,0:T(8,128)(2,1)S(1)} %collective-permute-done.12), channel_id=1, source_target_pairs={{0,1},{1,2},{2,3},{3,4},{4,5},{5,6},{6,7},{7,8},{8,9},{9,10},{10,1... | collective-permute-start | bytes 98312 | tf_op jit(solution)/shard_map/ppermute | solution.py:19
  351.4 4.8 copy-start.9
  351.4 142.5 %all-reduce.6.cloned.1.call-start = ((), (), s32[]{:S(2)}) async-start(), calls=%async_computation.8 | async-start | bytes 262144
  352.9 18.3 %copy-start.15 = (u32[32]{0:T(128)S(1)}, u32[32]{0:T(128)}, u32[]{:S(2)}) copy-start(u32[32]{0:T(128)} %constant.242) | copy-start | bytes 388
  353.8 203.4 %reduce-scatter.5.cloned.1.call-start = ((), (), s32[]{:S(2)}) async-start(), calls=%async_computation.6 | async-start | bytes 1114112 | tf_op jit(solution)/shard_map/reduce_scatter | solution.py:146
  357.8 10.0 %all-to-all-start.3 = ((bf16[16,2,192]{2,1,0:T(2,128)(2,1)}), bf16[16,2,192]{2,1,0:T(2,128)(2,1)S(1)}, u32[]{:S(2)}, u32[]{:S(2)}) async-start(bf16[16,2,192]{2,1,0:T(2,128)(2,1)} %reshape.354), calls=%async_computation.3 | async-start | bytes 32768 | tf_op jit(solution)/shard_map/all_to_all | solution.py:154
  367.7 10.0 %all-to-all-start.1 = ((bf16[2,16,384]{2,0,1:T(2,128)(2,1)}), bf16[2,16,384]{2,0,1:T(2,128)(2,1)S(1)}, u32[]{:S(2)}, u32[]{:S(2)}) async-start(bf16[2,16,384]{2,0,1:T(2,128)(2,1)} %bitcast_convert_fusion), calls=%async_computation.1 | async-start | bytes 49152 | tf_op jit(solution)/shard_map/all_to_all | solution.py:122
Sparse Core Ops, SparseCore 0:
  351.5 52.8 reduce-scatter.6
  407.9 85.9 all-reduce.5
  498.1 59.0 reduce-scatter.4
